TPU v7x, 256 devices: a whole 4x4x8 slice. The times are simulated.
256 devices in a mesh: pitch: 16 (over x_lo, z), radial: 8 (over y, core), axial: 2 (over x_hi).
Axes of the slice: x: 4 (x_hi: 2, x_lo: 2; x = x_hi * 2 + x_lo), y: 4, z: 8, core: 2. Of those that a mesh axis runs over, the one named last changes fastest.
Arguments:
- density: float32 [9, 4, 64, 2048], P(None, 'axial', 'radial', 'pitch'), may hold values from 0.5 to 2
- moments: float32 [9, 4, 4, 64, 2048], P(None, None, 'axial', 'radial', 'pitch'), may hold values from -6 to 6
- shifts: int32 [9], replicated, may hold values from 0 to 2047, as said below
Outputs:
- residual: float32 [9, 5, 4, 64, 2048], P(None, None, 'axial', 'radial', 'pitch')
- update: float32 [9, 5, 4, 64, 2048], P(None, None, 'axial', 'radial', 'pitch')
Inputs may be any that keep to these rules, and one draw needn't show every extreme that they name: `shifts`: every instance's offset lies in 0 to 2047 and some instance has offset 2048 - 1.
All inputs are finite; a program needn't handle non-finite values.
Results may differ from a plain program's by a relative error of at most 0.0005.
Values sent between devices are 32-bit elements; how exact they have to be, the bound alone decides.
No kernel may reach another device: no remote copies, remote signals or barrier semaphores. Data moves between devices by JAX's collectives and lax.ppermute only.
A program may use at most 192 MiB of HBM per device.

v0:
```python
import math
import jax
import jax.numpy as jnp
import numpy as np
from jax import lax
from jax.sharding import PartitionSpec as P

COEFFS = (0.75, -0.15, 1.0 / 60.0)
GAMMA_LESS = 0.4
HIGHEST = lax.Precision.HIGHEST


def padded_2(x, sides, width, wrap):
    for axis, dim in sides:
        devices, length = (lax.axis_size(axis), x.shape[dim])
        up = [(i, (i + 1) % devices) for i in range(devices if wrap else devices - 1)]
        down = [(j, i) for i, j in up]
        last = lax.slice_in_dim(x, length - width, length, axis=dim)
        leading = lax.slice_in_dim(x, 0, width, axis=dim)
        before = lax.ppermute(last, axis, up)
        after = lax.ppermute(leading, axis, down)
        x = jnp.concatenate([before, x, after], axis=dim)
    return x


def carried_in(x, axis, combine, identity, reverse):
    devices, position = (lax.axis_size(axis), lax.axis_index(axis))
    everything = jax.tree.map(lambda part: lax.all_gather(part, axis), x)
    start = jax.tree.map(
        lambda part, zero: jnp.broadcast_to(jnp.asarray(zero, part.dtype), part.shape), x, identity
    )

    def hop(k, before):
        at = devices - 1 - k if reverse else k
        reached = at > position if reverse else at < position
        new = combine(before, jax.tree.map(lambda part: part[at], everything))
        return jax.tree.map(lambda a, b: jnp.where(reached, a, b), new, before)

    return lax.fori_loop(0, devices, hop, start)


def from_partner(x, axis, apart):
    return lax.ppermute(x, axis, [(i, i ^ 1 << apart) for i in range(lax.axis_size(axis))])


def spectral_table(count):
    points = np.arange(count)
    spread = points[:, None] - points[None, :]
    nonzero = np.where(spread == 0, 1, spread)
    entries = 0.5 * np.where(spread % 2 == 0, 1.0, -1.0) / np.sin(np.pi * nonzero / count)
    return jnp.asarray(np.where(spread == 0, 0.0, entries), jnp.float32)


def fluxes(density, moments):
    axial_m = moments[:, 0]
    radial_m = moments[:, 1]
    pitch_m = moments[:, 2]
    energy = moments[:, 3]
    pressure = GAMMA_LESS * (
        energy - 0.5 * (axial_m * axial_m + radial_m * radial_m + pitch_m * pitch_m) / density
    )
    pitch_v = pitch_m / density
    radial_v = radial_m / density
    along_pitch = jnp.stack(
        [
            pitch_m,
            axial_m * pitch_v,
            radial_m * pitch_v,
            pitch_m * pitch_v + pressure,
            (energy + pressure) * pitch_v,
        ],
        axis=1,
    )
    along_radial = jnp.stack(
        [
            radial_m,
            axial_m * radial_v,
            radial_m * radial_v + pressure,
            pitch_m * radial_v,
            (energy + pressure) * radial_v,
        ],
        axis=1,
    )
    return (along_pitch, along_radial)


def stencil(padded, axis, length):
    summed = None
    for offset, weight in enumerate(COEFFS):
        reach = offset + 1
        ahead = lax.slice_in_dim(padded, 3 + reach, 3 + reach + length, axis=axis)
        behind = lax.slice_in_dim(padded, 3 - reach, 3 - reach + length, axis=axis)
        term = weight * (ahead - behind)
        summed = term if summed is None else summed + term
    return summed


def pitch_derivative(along_pitch):
    width = along_pitch.shape[-1]
    edges = jnp.concatenate([along_pitch[..., :3], along_pitch[..., width - 3 :]], axis=4)
    rims = padded_2(edges, (("pitch", 4),), 3, True)
    inner = None
    for offset, weight in enumerate(COEFFS):
        reach = offset + 1
        term = weight * (
            jnp.roll(along_pitch, -reach, axis=4) - jnp.roll(along_pitch, reach, axis=4)
        )
        inner = term if inner is None else inner + term
    left_strip = jnp.concatenate([rims[..., 0:3], along_pitch[..., :6]], axis=4)
    right_strip = jnp.concatenate([along_pitch[..., width - 6 :], rims[..., 9:12]], axis=4)
    left_cols = stencil(left_strip, 4, 3)
    right_cols = stencil(right_strip, 4, 3)
    pad_none = ((0, 0),) * 4
    left_full = jnp.pad(left_cols, pad_none + ((0, width - 3),))
    right_full = jnp.pad(right_cols, pad_none + ((width - 3, 0),))
    column = jnp.arange(width)
    return jnp.where(column < 3, left_full, jnp.where(column >= width - 3, right_full, inner))


def cut_rows(joined, starts, width):
    pieces = []
    for member in range(joined.shape[0]):
        opening = starts[member]
        pieces.append(lax.dynamic_slice_in_dim(joined[member], opening, width, axis=2))
    return jnp.stack(pieces, axis=0)


def carry_in(sums, backward, width, decay):
    count_p = lax.axis_size("pitch")
    place = lax.axis_index("pitch")
    step_log = width * math.log(decay)
    wrap_gain = 1.0 / (1.0 - decay ** (width * count_p))
    position = count_p - 1 - place if backward else place
    factor = jnp.full((1,), decay**width, jnp.float32)

    def combine(earlier, later):
        return (earlier[0] * later[0], later[1] + later[0] * earlier[1])

    scanned = carried_in(
        (factor, sums),
        "pitch",
        combine,
        (jnp.ones((1,), jnp.float32), jnp.zeros_like(sums)),
        backward,
    )
    weighted = sums * jnp.exp((count_p - 1 - position).astype(jnp.float32) * step_log)
    circuit = lax.psum(weighted, "pitch")
    return scanned[1] + jnp.exp(position.astype(jnp.float32) * step_log) * wrap_gain * circuit


def smooth(residual):
    width = residual.shape[-1]
    extent = width * lax.axis_size("pitch")
    smooth_eps = float(extent * extent // 16)
    decay = 2.0 * smooth_eps / (1.0 + 2.0 * smooth_eps + math.sqrt(1.0 + 4.0 * smooth_eps))
    points = np.arange(width)
    spacing = points[None, :] - points[:, None]
    lower = np.where(spacing >= 0, decay ** np.maximum(spacing, 0), 0.0)
    forward_table = jnp.asarray(lower, jnp.float32)
    backward_table = jnp.asarray(lower.T, jnp.float32)
    rising = jnp.asarray(decay ** (points + 1.0), jnp.float32)
    falling = jnp.asarray(decay ** (width - points + 0.0), jnp.float32)
    flat = residual.reshape(-1, width)
    first_pass = jnp.dot(flat, forward_table, precision=HIGHEST, preferred_element_type=jnp.float32)
    carried = carry_in(first_pass[:, -1], False, width, decay)
    swept = first_pass + carried[:, None] * rising[None, :]
    second_pass = jnp.dot(
        swept, backward_table, precision=HIGHEST, preferred_element_type=jnp.float32
    )
    carried_back = carry_in(second_pass[:, 0], True, width, decay)
    result = (second_pass + carried_back[:, None] * falling[None, :]) * (decay / smooth_eps)
    return result.reshape(residual.shape)


def local(density, moments, shifts):
    fields = jnp.concatenate([density[:, None], moments], axis=1)
    along_pitch, along_radial = fluxes(density, moments)
    count_p = lax.axis_size("pitch")
    place = lax.axis_index("pitch")
    width = density.shape[-1]
    planes = density.shape[1]
    padded_r = padded_2(along_radial, (("radial", 3),), 3, False)
    residual = pitch_derivative(along_pitch) + stencil(padded_r, 3, density.shape[2])
    residual = residual + jnp.einsum(
        "nm,mvarp->nvarp", spectral_table(fields.shape[0]), fields, precision=HIGHEST
    )
    stator = lax.axis_index("axial") == 1
    edge = jnp.where(stator, fields[:, :, 0], fields[:, :, planes - 1])
    facing = from_partner(edge, "axial", 0)
    extent = width * count_p
    offsets = jnp.where(stator, shifts, (extent - shifts) % extent)
    whole = lax.all_gather(facing, "pitch", axis=3, tiled=True)
    joined = jnp.concatenate([whole, whole], axis=3)
    aligned = cut_rows(joined, (place * width - offsets) % extent, width)
    penalty = aligned - edge
    target = jnp.where(stator, 0, planes - 1)
    chosen = (jnp.arange(planes) == target).astype(jnp.float32)
    residual = residual + penalty[:, :, None] * chosen[None, None, :, None, None]
    update = smooth(residual)
    return (residual, update)


def solution(mesh):
    in_specs = (P(None, "axial", "radial", "pitch"), P(None, None, "axial", "radial", "pitch"), P())
    out_specs = (
        P(None, None, "axial", "radial", "pitch"),
        P(None, None, "axial", "radial", "pitch"),
    )
    return jax.shard_map(local, mesh=mesh, in_specs=in_specs, out_specs=out_specs, check_vma=False)
```

profile of v0, /device:TPU:8, one launch (start us, length us, event | category | flops | bytes accessed | tf_op | source)
XLA Modules:
  0.0 391.4 jit_solution(6950493124615744178)
XLA Ops:
  9.4 3.1 collective-permute-start.4
  20.6 2.4 fusion.24
  23.0 2.2 copy.146
  25.2 2.4 bitcast_dynamic-update-slice_fusion.7
  27.6 2.8 bitcast_dynamic-update-slice_fusion.6
  31.1 2.2 copy.148
  34.7 2.9 bitcast_dynamic-update-slice_fusion.5
  38.2 3.0 bitcast_dynamic-update-slice_fusion.4
  44.8 4.0 %collective-permute-start.1 = (f32[9,5,2,8,3]{0,3,4,2,1:T(8,128)}, f32[9,5,2,8,3]{0,3,4,2,1:T(8,128)}, u32[]{:S(2)}, u32[]{:S(2)}) collective-permute-start(f32[9,5,2,8,3]{0,3,4,2,1:T(8,128)} %get-tuple-element.323), channel_id=1, source_target_pairs={{16,0},{32,16},{48,32},{64,48},{80,64},{96,80},{112,96},{128,112},... | collective-permute-start | bytes 25928 | tf_op jit(solution)/shard_map/ppermute | solution.py:21
  49.3 2.3 copy-done.1
  51.6 2.6 fusion.58
  54.1 3.5 copy.150
  59.6 2.2 copy.152
  61.8 2.4 collective-permute-start.3
  71.4 8.8 %fusion.53 = (f32[9,5,2,8,125]{0,3,4,2,1:T(8,128)}, f32[9,5,2,8,125]{0,3,4,2,1:T(8,128)}) fusion(f32[9,5,2,8,128]{0,3,4,2,1:T(8,128)} %get-tuple-element.336), kind=kLoop, calls=%fused_computation.138 | loop fusion | bytes 1440000 | tf_op jit(solution)/shard_map/jit(_roll_static)/slice | solution.py:106
  80.2 4.7 %fusion.55 = (f32[9,5,2,8,126]{0,3,4,2,1:T(8,128)}, f32[9,5,2,8,126]{0,3,4,2,1:T(8,128)}) fusion(f32[9,5,2,8,128]{0,3,4,2,1:T(8,128)S(1)} %bitcast.139), kind=kLoop, calls=%fused_computation.140 | loop fusion | bytes 1451520 | tf_op jit(solution)/shard_map/jit(_roll_static)/slice | solution.py:106
  84.9 4.6 %fusion.57 = (f32[9,5,2,8,127]{0,3,4,2,1:T(8,128)}, f32[9,5,2,8,127]{0,3,4,2,1:T(8,128)}) fusion(f32[9,5,2,8,128]{0,3,4,2,1:T(8,128)S(1)} %bitcast.139), kind=kLoop, calls=%fused_computation.142 | loop fusion | bytes 1463040 | tf_op jit(solution)/shard_map/jit(_roll_static)/slice | solution.py:106
  101.0 3.2 copy.156
  111.9 2.1 fusion.42
  114.0 2.7 copy.151
  116.7 3.3 copy.153
  120.0 14.6 %all-gather.4.cloned.1.call-done = f32[9,5,8,2048]{3,0,2,1:T(8,128)} async-done(((f32[9,5,8,128]{3,0,2,1:T(8,128)}), f32[9,5,8,2048]{3,0,2,1:T(8,128)}) %all-gather.4.cloned.1.call-update) | async-done | bytes 2949136 | tf_op jit(solution)/shard_map/all_gather | solution.py:192
  134.6 5.7 %constant_dynamic-update-slice_fusion.3 = f32[9,5,8,4096]{3,0,2,1:T(8,128)} fusion(f32[9,5,8,2048]{3,0,2,1:T(8,128)} %all-gather.4.cloned.1.call-done), kind=kLoop, calls=%fused_computation.110 | loop fusion | bytes 8192000
  140.3 3.0 constant_dynamic-update-slice_fusion.2
  143.3 20.9 %fusion.50 = (f32[1,5,8,4096]{3,0,2,1:T(1,128)}, f32[1,5,8,4096]{3,0,2,1:T(1,128)}, f32[1,5,8,4096]{3,0,2,1:T(1,128)}, f32[1,5,8,4096]{3,0,2,1:T(1,128)}, f32[1,...) fusion(f32[9,5,8,4096]{3,0,2,1:T(8,128)} %constant_dynamic-upda, ...), kind=kLoop, calls=%fused_computation.135 | loop fusion | bytes 11796480 | tf_op jit(solution)/shard_map/slice | solution.py:124
  174.0 3.3 copy.157
  177.3 35.9 %fusion.7 = f32[9,5,2,8,128]{0,3,4,2,1:T(8,128)} fusion(f32[9,5,2,8,128]{0,3,4,2,1:T(8,128)} %copy.156, f32[9,5,2,8,128]{0,3,4,2,1:T(8,128)} %copy-done.1, f32[9,5,2,3,128]{0,3,4,2,1:T(4,128)} %copy.153, f32[9,5,2,3,128]{0,3,4,2,1:T(4,128)S(1)} %copy.151, f32[9,5,2,8,1]{0,3,4,2,1:T(8,128)} %get-tuple-element.331, ...), kind=kLoop, calls=%fused_computation.21 | loop fusion | flops 3133440 | bytes 3796104 | tf_op jit(solution)/shard_map/add | solution.py:198
  213.2 3.4 copy.159
  217.8 63.2 %all-reduce.6 = (f32[11520]{0:T(1024)S(1)}, f32[16]{0:T(128)S(1)}, f32[720]{0:T(1024)S(1)}) all-reduce(f32[11520]{0:T(1024)S(1)} %dynamic-update-slice, f32[16]{0:T(128)S(1)} %dynamic-update-slice.1, f32[720]{0:T(1024)S(1)} %get-tuple-element.282), channel_id=2, replica_groups=mesh['pitch'=16,'radial'=8,'axial'=2] {'pitch'}, use_global_device_ids=true, to_apply=%add.2 | all-reduce | flops 12256 | bytes 98048
  281.1 20.6 %while.30 = (s32[]{:T(128)}, f32[720]{0:T(1024)S(1)}, s32[]{:T(128)}, f32[16,720]{1,0:T(8,128)S(1)}, f32[16,1]{0,1:T(1,128)S(1)}, /*index=5*/s32[]{:T(128)}, s32[]{:T(128)}) while((s32[]{:T(128)}, f32[720]{0:T(1024)S(1)}, s32[]{:T(128)}, f32[16,720]{1,0:T(8,128)S(1)}, f32[16,1]{0,1:T(1,128)S(1)}, /*index=5*/s32[]{:T(128)}, ...), condition=%wide.region_1.2_spmd.clone, body=%wide.region_0.1_spmd.clone.sunk | while | flops 2884 | bytes 14517 | solution.py:39
  302.8 59.9 %all-reduce.5 = (f32[11520]{0:T(1024)S(1)}, f32[720]{0:T(1024)S(1)}) all-reduce(f32[11520]{0:T(1024)S(1)} %dynamic-update-slice.2, f32[720]{0:T(1024)S(1)} %get-tuple-element.280), channel_id=3, replica_groups=mesh['pitch'=16,'radial'=8,'axial'=2] {'pitch'}, use_global_device_ids=true, to_apply=%add.4 | all-reduce | flops 12240 | bytes 97920
  362.9 20.7 %while.31 = (s32[]{:T(128)}, f32[720]{0:T(1024)S(1)}, s32[]{:T(128)}, f32[16,720]{1,0:T(8,128)S(1)}, f32[16,1]{0,1:T(1,128)S(1)}, /*index=5*/s32[]{:T(128)}, s32[]{:T(128)}, s32[]{:T(128)}, s32[]{:T(128)}) while((s32[]{:T(128)}, f32[720]{0:T(1024)S(1)}, s32[]{:T(128)}, f32[16,720]{1,0:T(8,128)S(1)}, f32[16,1]{0,1:T(1,128)S(1)}, ...), condition=%wide.region_4.5_spmd.clone, body=%wide.region_3.4_spmd.clone.sunk | while | flops 2888 | bytes 14579 | solution.py:39
  (193 shorter events, 81.5 us)
Async XLA Ops:
  7.2 127.5 %all-gather.4.cloned.1.call-start = ((), (), s32[]{:S(2)}) async-start(), calls=%async_computation | async-start | bytes 5570560 | tf_op jit(solution)/shard_map/all_gather | solution.py:192
  8.4 4.2 %copy-start.5 = (f32[9,4,2,8,128]{4,0,3,2,1:T(8,128)}, f32[9,4,2,8,128]{4,0,3,2,1:T(8,128)S(1)}, u32[]{:S(2)}) copy-start(f32[9,4,2,8,128]{4,0,3,2,1:T(8,128)S(1)} %copy.155) | copy-start | bytes 884740
  9.4 3.2 copy-start.8
  9.4 25.2 %collective-permute-start.4 = (f32[9,5,8,128]{3,0,2,1:T(8,128)S(1)}, f32[9,5,8,128]{3,0,2,1:T(8,128)}, u32[]{:S(2)}, u32[]{:S(2)}) collective-permute-start(f32[9,5,8,128]{3,0,2,1:T(8,128)S(1)} %bitcast.141), channel_id=1, source_target_pairs={{0,1},{1,0},{2,3},{3,2},{4,5},{5,4},{6,7},{7,6},{8,9},{9,8},{10,11... | collective-permute-start | bytes 552968 | tf_op jit(solution)/shard_map/ppermute | solution.py:43
  25.2 5.2 %copy-start.9 = (f32[9,2,8,128]{3,2,1,0:T(8,128)S(1)}, f32[9,2,8,128]{3,2,1,0:T(8,128)}, u32[]{:S(2)}) copy-start(f32[9,2,8,128]{3,2,1,0:T(8,128)} %param.12) | copy-start | bytes 221188
  25.2 5.2 %copy-start.10 = (f32[9,2,8,128]{3,2,1,0:T(8,128)S(1)}, f32[9,2,8,128]{3,2,1,0:T(8,128)}, u32[]{:S(2)}) copy-start(f32[9,2,8,128]{3,2,1,0:T(8,128)} %copy.146) | copy-start | bytes 221188
  34.7 3.5 copy-start
  38.2 10.7 %copy-start.3 = (f32[9,2,8,128]{0,2,3,1:T(8,128)S(1)}, f32[9,2,8,128]{0,2,3,1:T(8,128)}, u32[]{:S(2)}) copy-start(f32[9,2,8,128]{0,2,3,1:T(8,128)} %copy.148) | copy-start | bytes 221188
  38.2 10.7 %copy-start.4 = (f32[9,1,2,8,128]{0,3,4,2,1:T(8,128)S(1)}, f32[9,1,2,8,128]{0,3,4,2,1:T(8,128)}, u32[]{:S(2)}) copy-start(f32[9,1,2,8,128]{0,3,4,2,1:T(8,128)} %copy.164) | copy-start | bytes 221188
  42.9 69.0 %collective-permute-start = (f32[9,5,2,8,3]{0,3,4,2,1:T(8,128)}, f32[9,5,2,8,3]{0,3,4,2,1:T(8,128)}, u32[]{:S(2)}, u32[]{:S(2)}) collective-permute-start(f32[9,5,2,8,3]{0,3,4,2,1:T(8,128)} %get-tuple-element.322), channel_id=1, source_target_pairs={{0,16},{16,32},{32,48},{48,64},{64,80},{80,96},{96,112},{112,128},... | collective-permute-start | bytes 25928 | tf_op jit(solution)/shard_map/ppermute | solution.py:20
  44.8 67.1 %collective-permute-start.1 = (f32[9,5,2,8,3]{0,3,4,2,1:T(8,128)}, f32[9,5,2,8,3]{0,3,4,2,1:T(8,128)}, u32[]{:S(2)}, u32[]{:S(2)}) collective-permute-start(f32[9,5,2,8,3]{0,3,4,2,1:T(8,128)} %get-tuple-element.323), channel_id=1, source_target_pairs={{16,0},{32,16},{48,32},{64,48},{80,64},{96,80},{112,96},{128,112},... | collective-permute-start | bytes 25928 | tf_op jit(solution)/shard_map/ppermute | solution.py:21
  49.3 2.3 copy-start.1
  54.1 10.7 %copy-start.15 = (s32[9]{0:T(128)S(1)}, s32[9]{0:T(128)}, u32[]{:S(2)}) copy-start(s32[9]{0:T(128)} %param.14) | copy-start | bytes 112
  54.1 14.4 %copy-start.6 = (f32[9,4,2,8,128]{4,0,3,2,1:T(8,128)S(1)}, f32[9,4,2,8,128]{4,0,3,2,1:T(8,128)}, u32[]{:S(2)}) copy-start(f32[9,4,2,8,128]{4,0,3,2,1:T(8,128)} %copy-done.5) | copy-start | bytes 884740
  57.6 56.4 %collective-permute-start.2 = (f32[9,5,2,3,128]{4,2,3,1,0:T(2,128)}, f32[9,5,2,3,128]{4,2,3,1,0:T(2,128)}, u32[]{:S(2)}, u32[]{:S(2)}) collective-permute-start(f32[9,5,2,3,128]{4,2,3,1,0:T(2,128)} %copy.150), channel_id=1, source_target_pairs={{2,0},{4,2},{6,4},{8,6},{10,8},{12,10},{14,12},{3,1},{5,3},{7,5},{... | collective-permute-start | bytes 414728 | tf_op jit(solution)/shard_map/ppermute | solution.py:21
  61.8 54.9 %collective-permute-start.3 = (f32[9,5,2,3,128]{4,2,3,1,0:T(2,128)}, f32[9,5,2,3,128]{4,2,3,1,0:T(2,128)}, u32[]{:S(2)}, u32[]{:S(2)}) collective-permute-start(f32[9,5,2,3,128]{4,2,3,1,0:T(2,128)} %copy.152), channel_id=1, source_target_pairs={{0,2},{2,4},{4,6},{6,8},{8,10},{10,12},{12,14},{1,3},{3,5},{5,7},{... | collective-permute-start | bytes 414728 | tf_op jit(solution)/shard_map/ppermute | solution.py:20
  70.1 10.1 %slice-start = ((s8[5242880]{0:T(1024)(128)(4,1)}), s8[4194304]{0:T(1024)(128)(4,1)S(1)}, s32[]{:S(2)}) async-start(s8[5242880]{0:T(1024)(128)(4,1)} %bitcast.138), calls=%async_computation.1 | async-start | bytes 8388608
  71.4 8.8 %slice-start.1 = ((s8[5242880]{0:T(1024)(128)(4,1)}), s8[1048576]{0:T(1024)(128)(4,1)S(1)}, s32[]{:S(2)}) async-start(s8[5242880]{0:T(1024)(128)(4,1)} %bitcast.138), calls=%async_computation.2 | async-start | bytes 2097152
  89.5 20.3 %copy-start.17 = (u32[256]{0:T(256)S(1)}, u32[256]{0:T(256)}, u32[]{:S(2)}) copy-start(u32[256]{0:T(256)} %constant.161) | copy-start | bytes 3076
  134.6 5.7 %copy-start.2 = (f32[9,5,8,2048]{3,0,2,1:T(8,128)S(1)}, f32[9,5,8,2048]{3,0,2,1:T(8,128)}, u32[]{:S(2)}) copy-start(f32[9,5,8,2048]{3,0,2,1:T(8,128)} %all-gather.4.cloned.1.call-done) | copy-start | bytes 8847364
  143.3 34.0 %copy-start.11 = (f32[9,5,2,8,1]{0,3,4,2,1:T(8,128)S(1)}, f32[9,5,2,8,1]{0,3,4,2,1:T(8,128)}, u32[]{:S(2)}) copy-start(f32[9,5,2,8,1]{0,3,4,2,1:T(8,128)} %get-tuple-element.330) | copy-start | bytes 8644
  213.2 3.4 copy-start.12
  213.2 88.5 %copy-start.13 = (f32[128,128]{1,0:T(8,128)S(1)}, f32[128,128]{1,0:T(8,128)}, u32[]{:S(2)}) copy-start(f32[128,128]{1,0:T(8,128)} %constant.152.clone) | copy-start | bytes 196612
  213.2 88.5 %copy-start.16 = (f32[128]{0:T(128)S(1)}, f32[128]{0:T(128)}, u32[]{:S(2)}) copy-start(f32[128]{0:T(128)} %constant.153.clone) | copy-start | bytes 1540
  213.2 170.4 %copy-start.14 = (f32[128]{0:T(128)S(1)}, f32[128]{0:T(128)}, u32[]{:S(2)}) copy-start(f32[128]{0:T(128)} %constant.154.clone) | copy-start | bytes 1540
  216.6 167.9 %copy-start.7 = (f32[9,5,2,8,128]{4,3,2,1,0:T(8,128)}, f32[9,5,2,8,128]{4,3,2,1,0:T(8,128)S(1)}, u32[]{:S(2)}) copy-start(f32[9,5,2,8,128]{4,3,2,1,0:T(8,128)S(1)} %copy.159) | copy-start | bytes 1105924
Sparse Core Ops, SparseCore 0:
  34.8 99.7 all-gather.3
where the time goes:
time: 393 us; the launch traced here: 391 us
  local copies, waits for them, and re-layouts  128 us (33%)
  blocking collectives  123 us (31%)
  other arithmetic  77 us (20%)
  between operations  31.6 us (8%)
  waiting for transfers between devices  14.6 us (4%)
  starting transfers between devices  13.3 us (3%)
    unnamed x2, blocking collectives  123 us
    add x1, other arithmetic, local(): residual + penalty[:, :, None] * chosen[None, None, :, None, None]  35.9 us
    unnamed x58, local copies, waits for them, and re-layouts  23.9 us
    slice x5, local copies, waits for them, and re-layouts, pitch_derivative(): jnp.roll(along_pitch, reach, axis=4)  21.1 us
    slice x1, local copies, waits for them, and re-layouts, cut_rows(): joined[member]  20.9 us
    select_n x32, other arithmetic, hop(): return jax.tree.map(lambda a, b: jnp.where(reached, a, b), new, before)  20.8 us
    dynamic_slice x64, local copies, waits for them, and re-layouts, hop(): new = combine(before, jax.tree.map(lambda part: part[at], everything))  19.5 us
    all_gather x1, waiting for transfers between devices, local(): whole = lax.all_gather(facing, 'pitch', axis=3, tiled=True)  14.6 us
  transfers between devices with their start and end apart: 6, of which 1 were waited for; matrix products, arithmetic and copies ran while one was open for 20% of the time, Pallas kernels for 0%

commit v1 on v0

--- a/solution.py
+++ b/solution.py
@@ -189,7 +189,10 @@
     facing = from_partner(edge, "axial", 0)
     extent = width * count_p
     offsets = jnp.where(stator, shifts, (extent - shifts) % extent)
-    whole = lax.all_gather(facing, "pitch", axis=3, tiled=True)
+    size = lax.axis_size("pitch")
+    blocks = jnp.stack([facing for _ in range(size)])
+    blocks = lax.all_to_all(blocks, "pitch", split_axis=0, concat_axis=0)
+    whole = jnp.concatenate(blocks, axis=3)
     joined = jnp.concatenate([whole, whole], axis=3)
     aligned = cut_rows(joined, (place * width - offsets) % extent, width)
     penalty = aligned - edge

time: 393 us -> 347 us (0.88)
  local copies, waits for them, and re-layouts: 128 us -> 103 us
  waiting for transfers between devices: 14.6 us -> 0.02 us
  between operations: 31.6 us -> 18.4 us
  starting transfers between devices: 13.3 us -> 20.4 us
    slice x1, local copies, waits for them, and re-layouts: 20.9 us -> 0.67 us  [cut_rows(): joined[member]]
    all_gather x1 -> x0, waiting for transfers between devices: 14.6 us -> none  [local(): whole = lax.all_gather(facing, 'pitch', axis=3, tiled=True)]
    all_to_all x0 -> x1, starting transfers between devices: none -> 8.64 us  [local(): blocks = lax.all_to_all(blocks, 'pitch', split_axis=0, concat_axis=0)]
    another operation x6 -> x1, local copies, waits for them, and re-layouts: 9.02 us -> 1.82 us  [cut_rows(): return jnp.stack(pieces, axis=0)]
    unnamed x58 -> x52, local copies, waits for them, and re-layouts: 23.9 us -> 17.4 us
    slice x2, local copies, waits for them, and re-layouts: 6.06 us -> 10 us  [padded_2(): leading = lax.slice_in_dim(x, 0, width, axis=dim)]
  transfers between devices with their start and end apart: 6 -> 6, of which waited for: 1 -> 0; matrix products, arithmetic and copies ran while one was open for 20% -> 24% of each run, Pallas kernels for 0% -> 0%
where the time goes in v1:
time: 347 us; the launch traced here: 344 us
  blocking collectives  122 us (35%)
  local copies, waits for them, and re-layouts  103 us (30%)
  other arithmetic  77.7 us (22%)
  starting transfers between devices  20.4 us (6%)
  between operations  18.4 us (5%)
    unnamed x2, blocking collectives  122 us
    add x1, other arithmetic, local(): residual + penalty[:, :, None] * chosen[None, None, :, None, None]  35.9 us
    slice x5, local copies, waits for them, and re-layouts, pitch_derivative(): jnp.roll(along_pitch, reach, axis=4)  20.9 us
    select_n x32, other arithmetic, hop(): return jax.tree.map(lambda a, b: jnp.where(reached, a, b), new, before)  20.8 us
    dynamic_slice x64, local copies, waits for them, and re-layouts, hop(): new = combine(before, jax.tree.map(lambda part: part[at], everything))  19.5 us
    unnamed x52, local copies, waits for them, and re-layouts  17.4 us
    slice x2, local copies, waits for them, and re-layouts, padded_2(): leading = lax.slice_in_dim(x, 0, width, axis=dim)  10 us
    unnamed x7, other arithmetic  9.26 us
  transfers between devices with their start and end apart: 6, of which 0 were waited for; matrix products, arithmetic and copies ran while one was open for 24% of the time, Pallas kernels for 0%

profile of v1, /device:TPU:8, one launch (start us, length us, event | category | flops | bytes accessed | tf_op | source)
XLA Modules:
  0.0 344.4 jit_solution(3395495685797877515)
XLA Ops:
  2.8 3.1 collective-permute-start.4
  14.1 2.3 fusion.24
  16.4 2.2 copy.174
  18.6 2.4 bitcast_dynamic-update-slice_fusion.9
  21.0 2.8 bitcast_dynamic-update-slice_fusion.8
  24.4 2.3 copy.176
  30.8 8.6 %all-to-all-start = ((f32[16,9,5,8,128]{4,3,2,1,0:T(8,128)}), f32[16,9,5,8,128]{4,3,2,1,0:T(8,128)}, u32[]{:S(2)}, u32[]{:S(2)}) async-start(f32[16,9,5,8,128]{4,3,2,1,0:T(8,128)} %stack.89), calls=%async_computation | async-start | bytes 5898240 | tf_op jit(solution)/shard_map/all_to_all | solution.py:194
  39.5 2.9 bitcast_dynamic-update-slice_fusion.7
  42.4 1.8 bitcast_dynamic-update-slice_fusion.6
  45.8 1.9 collective-permute-start
  47.7 2.3 collective-permute-start.1
  52.5 6.5 %fusion.58 = (f32[9,5,2,3,128]{0,3,4,2,1:T(4,128)}, f32[9,5,2,3,128]{0,3,4,2,1:T(4,128)S(1)}) fusion(f32[9,5,2,8,128]{0,3,4,2,1:T(8,128)} %bitcast_dynamic-update-slice_fusion.2), kind=kLoop, calls=%fused_computation.143 | loop fusion | bytes 552960 | tf_op jit(solution)/shard_map/slice | solution.py:19
  59.0 3.5 %copy.178 = f32[9,5,2,3,128]{4,2,3,1,0:T(2,128)} copy(f32[9,5,2,3,128]{0,3,4,2,1:T(4,128)} %get-tuple-element.336) | data formatting | bytes 276480 | tf_op jit(solution)/shard_map/slice | solution.py:19
  62.5 1.9 collective-permute-start.2
  64.4 2.2 copy.180
  66.7 2.6 collective-permute-start.3
  76.5 8.7 %fusion.53 = (f32[9,5,2,8,125]{0,3,4,2,1:T(8,128)}, f32[9,5,2,8,125]{0,3,4,2,1:T(8,128)}) fusion(f32[9,5,2,8,128]{0,3,4,2,1:T(8,128)} %get-tuple-element.338), kind=kLoop, calls=%fused_computation.138 | loop fusion | bytes 1440000 | tf_op jit(solution)/shard_map/jit(_roll_static)/slice | solution.py:106
  85.2 4.6 %fusion.55 = (f32[9,5,2,8,126]{0,3,4,2,1:T(8,128)}, f32[9,5,2,8,126]{0,3,4,2,1:T(8,128)}) fusion(f32[9,5,2,8,128]{0,3,4,2,1:T(8,128)S(1)} %bitcast.139), kind=kLoop, calls=%fused_computation.140 | loop fusion | bytes 1451520 | tf_op jit(solution)/shard_map/jit(_roll_static)/slice | solution.py:106
  89.7 4.6 %fusion.57 = (f32[9,5,2,8,127]{0,3,4,2,1:T(8,128)}, f32[9,5,2,8,127]{0,3,4,2,1:T(8,128)}) fusion(f32[9,5,2,8,128]{0,3,4,2,1:T(8,128)S(1)} %bitcast.139), kind=kLoop, calls=%fused_computation.142 | loop fusion | bytes 1463040 | tf_op jit(solution)/shard_map/jit(_roll_static)/slice | solution.py:106
  106.1 3.1 copy.184
  116.8 2.1 fusion.42
  118.9 2.7 copy.179
  121.6 3.4 copy.181
  124.9 2.2 bitcast_dynamic-update-slice_fusion
  127.1 2.2 bitcast_dynamic-update-slice_fusion.1
  135.5 3.2 copy.187
  138.7 35.9 %fusion.7 = f32[9,5,2,8,128]{0,3,4,2,1:T(8,128)} fusion(f32[9,5,2,8,128]{0,3,4,2,1:T(8,128)} %copy.184, f32[9,5,2,8,128]{0,3,4,2,1:T(8,128)} %bitcast_dynamic-update-slice_fusion.2, f32[9,5,2,3,128]{0,3,4,2,1:T(4,128)} %copy.181, f32[9,5,2,3,128]{0,3,4,2,1:T(4,128)S(1)} %copy.179, f32[9,5,2,8,1]{0,3,4,2,1:T(8,128)} %get-tuple-element.333, ...), kind=kLoop, calls=%fused_computation.21 | loop fusion | flops 3133440 | bytes 3796104 | tf_op jit(solution)/shard_map/add | solution.py:201
  174.7 3.4 copy.189
  179.2 61.7 %all-reduce.6 = (f32[11520]{0:T(1024)S(1)}, f32[16]{0:T(128)S(1)}, f32[720]{0:T(1024)S(1)}) all-reduce(f32[11520]{0:T(1024)S(1)} %dynamic-update-slice, f32[16]{0:T(128)S(1)} %dynamic-update-slice.1, f32[720]{0:T(1024)S(1)} %get-tuple-element.284), channel_id=2, replica_groups=mesh['pitch'=16,'radial'=8,'axial'=2] {'pitch'}, use_global_device_ids=true, to_apply=%add.2 | all-reduce | flops 12256 | bytes 98048
  241.0 20.6 %while.30 = (s32[]{:T(128)}, f32[720]{0:T(1024)S(1)}, s32[]{:T(128)}, f32[16,720]{1,0:T(8,128)S(1)}, f32[16,1]{0,1:T(1,128)S(1)}, /*index=5*/s32[]{:T(128)}, s32[]{:T(128)}) while((s32[]{:T(128)}, f32[720]{0:T(1024)S(1)}, s32[]{:T(128)}, f32[16,720]{1,0:T(8,128)S(1)}, f32[16,1]{0,1:T(1,128)S(1)}, /*index=5*/s32[]{:T(128)}, ...), condition=%wide.region_1.2_spmd.clone, body=%wide.region_0.1_spmd.clone.sunk | while | flops 2884 | bytes 14517 | solution.py:39
  262.7 59.9 %all-reduce.5 = (f32[11520]{0:T(1024)S(1)}, f32[720]{0:T(1024)S(1)}) all-reduce(f32[11520]{0:T(1024)S(1)} %dynamic-update-slice.2, f32[720]{0:T(1024)S(1)} %get-tuple-element.282), channel_id=3, replica_groups=mesh['pitch'=16,'radial'=8,'axial'=2] {'pitch'}, use_global_device_ids=true, to_apply=%add.4 | all-reduce | flops 12240 | bytes 97920
  322.8 20.7 %while.31 = (s32[]{:T(128)}, f32[720]{0:T(1024)S(1)}, s32[]{:T(128)}, f32[16,720]{1,0:T(8,128)S(1)}, f32[16,1]{0,1:T(1,128)S(1)}, /*index=5*/s32[]{:T(128)}, s32[]{:T(128)}, s32[]{:T(128)}, s32[]{:T(128)}) while((s32[]{:T(128)}, f32[720]{0:T(1024)S(1)}, s32[]{:T(128)}, f32[16,720]{1,0:T(8,128)S(1)}, f32[16,1]{0,1:T(1,128)S(1)}, ...), condition=%wide.region_4.5_spmd.clone, body=%wide.region_3.4_spmd.clone.sunk | while | flops 2888 | bytes 14579 | solution.py:39
  (188 shorter events, 78.0 us)
Async XLA Ops:
  1.8 4.2 %copy-start.2 = (f32[9,4,2,8,128]{4,0,3,2,1:T(8,128)}, f32[9,4,2,8,128]{4,0,3,2,1:T(8,128)S(1)}, u32[]{:S(2)}) copy-start(f32[9,4,2,8,128]{4,0,3,2,1:T(8,128)S(1)} %copy.183) | copy-start | bytes 884740
  2.8 3.2 copy-start.5
  2.8 25.2 %collective-permute-start.4 = (f32[9,5,8,128]{3,0,2,1:T(8,128)S(1)}, f32[9,5,8,128]{3,0,2,1:T(8,128)}, u32[]{:S(2)}, u32[]{:S(2)}) collective-permute-start(f32[9,5,8,128]{3,0,2,1:T(8,128)S(1)} %bitcast.141), channel_id=1, source_target_pairs={{0,1},{1,0},{2,3},{3,2},{4,5},{5,4},{6,7},{7,6},{8,9},{9,8},{10,11... | collective-permute-start | bytes 552968 | tf_op jit(solution)/shard_map/ppermute | solution.py:43
  18.6 5.2 %copy-start.6 = (f32[9,2,8,128]{3,2,1,0:T(8,128)S(1)}, f32[9,2,8,128]{3,2,1,0:T(8,128)}, u32[]{:S(2)}) copy-start(f32[9,2,8,128]{3,2,1,0:T(8,128)} %param.12) | copy-start | bytes 221188
  18.6 5.2 %copy-start.7 = (f32[9,2,8,128]{3,2,1,0:T(8,128)S(1)}, f32[9,2,8,128]{3,2,1,0:T(8,128)}, u32[]{:S(2)}) copy-start(f32[9,2,8,128]{3,2,1,0:T(8,128)} %copy.174) | copy-start | bytes 221188
  30.8 94.1 %all-to-all-start = ((f32[16,9,5,8,128]{4,3,2,1,0:T(8,128)}), f32[16,9,5,8,128]{4,3,2,1,0:T(8,128)}, u32[]{:S(2)}, u32[]{:S(2)}) async-start(f32[16,9,5,8,128]{4,3,2,1,0:T(8,128)} %stack.89), calls=%async_computation | async-start | bytes 5898240 | tf_op jit(solution)/shard_map/all_to_all | solution.py:194
  39.5 2.9 copy-start
  39.5 2.9 copy-start.1
  45.8 70.9 %collective-permute-start = (f32[9,5,2,8,3]{0,3,4,2,1:T(8,128)}, f32[9,5,2,8,3]{0,3,4,2,1:T(8,128)}, u32[]{:S(2)}, u32[]{:S(2)}) collective-permute-start(f32[9,5,2,8,3]{0,3,4,2,1:T(8,128)} %get-tuple-element.324), channel_id=1, source_target_pairs={{0,16},{16,32},{32,48},{48,64},{64,80},{80,96},{96,112},{112,128},... | collective-permute-start | bytes 25928 | tf_op jit(solution)/shard_map/ppermute | solution.py:20
  47.7 69.1 %collective-permute-start.1 = (f32[9,5,2,8,3]{0,3,4,2,1:T(8,128)}, f32[9,5,2,8,3]{0,3,4,2,1:T(8,128)}, u32[]{:S(2)}, u32[]{:S(2)}) collective-permute-start(f32[9,5,2,8,3]{0,3,4,2,1:T(8,128)} %get-tuple-element.325), channel_id=1, source_target_pairs={{16,0},{32,16},{48,32},{64,48},{80,64},{96,80},{112,96},{128,112},... | collective-permute-start | bytes 25928 | tf_op jit(solution)/shard_map/ppermute | solution.py:21
  59.0 10.8 %copy-start.12 = (s32[9]{0:T(128)S(1)}, s32[9]{0:T(128)}, u32[]{:S(2)}) copy-start(s32[9]{0:T(128)} %param.14) | copy-start | bytes 112
  59.0 14.6 %copy-start.3 = (f32[9,4,2,8,128]{4,0,3,2,1:T(8,128)S(1)}, f32[9,4,2,8,128]{4,0,3,2,1:T(8,128)}, u32[]{:S(2)}) copy-start(f32[9,4,2,8,128]{4,0,3,2,1:T(8,128)} %copy-done.2) | copy-start | bytes 884740
  62.5 56.4 %collective-permute-start.2 = (f32[9,5,2,3,128]{4,2,3,1,0:T(2,128)}, f32[9,5,2,3,128]{4,2,3,1,0:T(2,128)}, u32[]{:S(2)}, u32[]{:S(2)}) collective-permute-start(f32[9,5,2,3,128]{4,2,3,1,0:T(2,128)} %copy.178), channel_id=1, source_target_pairs={{2,0},{4,2},{6,4},{8,6},{10,8},{12,10},{14,12},{3,1},{5,3},{7,5},{... | collective-permute-start | bytes 414728 | tf_op jit(solution)/shard_map/ppermute | solution.py:21
  66.7 54.9 %collective-permute-start.3 = (f32[9,5,2,3,128]{4,2,3,1,0:T(2,128)}, f32[9,5,2,3,128]{4,2,3,1,0:T(2,128)}, u32[]{:S(2)}, u32[]{:S(2)}) collective-permute-start(f32[9,5,2,3,128]{4,2,3,1,0:T(2,128)} %copy.180), channel_id=1, source_target_pairs={{0,2},{2,4},{4,6},{6,8},{8,10},{10,12},{12,14},{1,3},{3,5},{5,7},{... | collective-permute-start | bytes 414728 | tf_op jit(solution)/shard_map/ppermute | solution.py:20
  75.2 10.0 %slice-start = ((s8[5242880]{0:T(1024)(128)(4,1)}), s8[4194304]{0:T(1024)(128)(4,1)S(1)}, s32[]{:S(2)}) async-start(s8[5242880]{0:T(1024)(128)(4,1)} %bitcast.138), calls=%async_computation.1 | async-start | bytes 8388608
  76.4 8.7 %slice-start.1 = ((s8[5242880]{0:T(1024)(128)(4,1)}), s8[1048576]{0:T(1024)(128)(4,1)S(1)}, s32[]{:S(2)}) async-start(s8[5242880]{0:T(1024)(128)(4,1)} %bitcast.138), calls=%async_computation.2 | async-start | bytes 2097152
  94.4 20.6 %copy-start.14 = (u32[256]{0:T(256)S(1)}, u32[256]{0:T(256)}, u32[]{:S(2)}) copy-start(u32[256]{0:T(256)} %constant.161) | copy-start | bytes 3076
  129.3 9.4 %copy-start.8 = (f32[9,5,2,8,1]{0,3,4,2,1:T(8,128)S(1)}, f32[9,5,2,8,1]{0,3,4,2,1:T(8,128)}, u32[]{:S(2)}) copy-start(f32[9,5,2,8,1]{0,3,4,2,1:T(8,128)} %get-tuple-element.332) | copy-start | bytes 8644
  174.6 3.4 copy-start.9
  174.6 87.0 %copy-start.10 = (f32[128,128]{1,0:T(8,128)S(1)}, f32[128,128]{1,0:T(8,128)}, u32[]{:S(2)}) copy-start(f32[128,128]{1,0:T(8,128)} %constant.152.clone) | copy-start | bytes 196612
  174.6 87.0 %copy-start.13 = (f32[128]{0:T(128)S(1)}, f32[128]{0:T(128)}, u32[]{:S(2)}) copy-start(f32[128]{0:T(128)} %constant.153.clone) | copy-start | bytes 1540
  174.6 168.9 %copy-start.11 = (f32[128]{0:T(128)S(1)}, f32[128]{0:T(128)}, u32[]{:S(2)}) copy-start(f32[128]{0:T(128)} %constant.154.clone) | copy-start | bytes 1540
  178.0 166.4 %copy-start.4 = (f32[9,5,2,8,128]{4,3,2,1,0:T(8,128)}, f32[9,5,2,8,128]{4,3,2,1,0:T(8,128)S(1)}, u32[]{:S(2)}) copy-start(f32[9,5,2,8,128]{4,3,2,1,0:T(8,128)S(1)} %copy.189) | copy-start | bytes 1105924
